TPU v7x, 1024 devices: a whole 4x8x16 slice. The times are simulated.
1024 devices in a mesh: dp: 64 (over y, x, core), replica: 16 (over z).
Axes of the slice: x: 4, y: 8, z: 16, core: 2. Of those that a mesh axis runs over, the one named last changes fastest.
Arguments:
- tokens: bfloat16 [16, 8192, 1024], P('replica', 'dp'), may hold values from -16 to 16
- user_of_row: int32 [16, 8192], P('replica'), may hold values from 0 to 255, as said below
- proj_weight: bfloat16 [1024, 1536], replicated
- norm_gain: float32 [512], replicated, may hold values from 0.5 to 1.5
- grad_out: bfloat16 [16, 16384, 512], P('replica', 'dp'), may hold values from -6 to 6
Outputs:
- attended: bfloat16 [16, 16384, 512], P('replica', 'dp')
- grad_tokens: bfloat16 [16, 8192, 1024], P('replica', 'dp')
- grad_weight: float32 [1024, 1536], P('dp')
Inputs may be any that keep to these rules, and one draw needn't show every extreme that they name: `user_of_row`: user u belongs to owner u // 4. Among the 128 rows of one source device in one batch at most 4 belong to users of any one owner, and in every batch one owner gets exactly 4 rows from every source.
All inputs are finite; a program needn't handle non-finite values.
Results may differ from a plain program's by a relative error of at most 0.0068.
Values may be sent and summed in bfloat16 or wider, within the bound.
A program may use at most 64 MiB of HBM per device.

v0:
```python
import jax
import jax.numpy as jnp
from jax import lax
from jax.sharding import PartitionSpec as P

HEADS = 4
HEAD_DIM = 128
UPO = 4


def silu_grad(preact):
    sigmoid_p = jax.nn.sigmoid(preact)
    return sigmoid_p * (1.0 + preact * (1.0 - sigmoid_p))


def attend(activated, gain, slot_user, slot_order):
    slot_total = activated.shape[0]
    split_acts = activated.astype(jnp.float32).reshape(slot_total, 3, HEADS, HEAD_DIM)
    queries = split_acts[:, 0]
    keys_h = split_acts[:, 1]
    values = split_acts[:, 2]
    scores = jnp.einsum(
        "qhd,khd->hqk", queries, keys_h, precision=lax.Precision.HIGHEST
    ) * HEAD_DIM ** (-0.5)
    visible = (
        (slot_user[:, None] == slot_user[None, :])
        & (slot_order[None, :] <= slot_order[:, None])
        & (slot_user[:, None] >= 0)
    )
    weights = jnp.where(visible[None], jax.nn.silu(scores), 0.0)
    mixed = jnp.einsum("hqk,khd->qhd", weights, values, precision=lax.Precision.HIGHEST).reshape(
        slot_total, HEADS * HEAD_DIM
    )
    mean_row = jnp.mean(mixed, axis=1, keepdims=True)
    centered = mixed - mean_row
    variance = jnp.mean(centered * centered, axis=1, keepdims=True)
    return centered * lax.rsqrt(variance + 1e-06) * gain


def block_pass(activated, gain, slot_user, slot_order, cotangent):

    def forward(acts):
        return attend(acts, gain, slot_user, slot_order)

    normed, pull = jax.vjp(forward, activated)
    (d_acts,) = pull(cotangent.astype(jnp.float32))
    return (normed.astype(jnp.bfloat16), d_acts)


def body(tokens, user_of_row, proj_weight, norm_gain, grad_out):
    peer_count = lax.axis_size("dp")
    self_index = lax.axis_index("dp")
    row_count = tokens.shape[1]
    width = proj_weight.shape[0]
    capacity = 2 * row_count // peer_count
    slot_count = peer_count * capacity
    routing = user_of_row[0]
    owners = (routing // UPO).reshape(peer_count, row_count)
    peer_ids = jnp.arange(peer_count, dtype=jnp.int32)
    inbound = (owners == self_index).astype(jnp.int32)
    in_rank = jnp.cumsum(inbound, axis=1) - 1
    matches = (
        (inbound[:, None, :] == 1)
        & (in_rank[:, None, :] == jnp.arange(capacity, dtype=jnp.int32)[None, :, None])
    ).astype(jnp.int32)
    users_src = routing.reshape(peer_count, row_count)
    slot_user = jnp.sum(matches * (users_src[:, None, :] + 1), axis=2).reshape(slot_count) - 1
    order_src = jnp.arange(peer_count * row_count, dtype=jnp.int32).reshape(peer_count, row_count)
    slot_order = jnp.sum(matches * order_src[:, None, :], axis=2).reshape(slot_count)
    own_owner = lax.dynamic_slice_in_dim(owners, self_index, 1, 0)[0]
    to_peer = (own_owner[:, None] == peer_ids[None, :]).astype(jnp.int32)
    out_rank = jnp.sum(jnp.cumsum(to_peer, axis=0) * to_peer, axis=1) - 1
    position = own_owner * capacity + out_rank
    rows_x = tokens[0]
    cotangent = grad_out[0]
    contract_cols = (((1,), (1,)), ((), ()))
    contract_rows = (((0,), (0,)), ((), ()))
    outgoing = jnp.zeros((slot_count, width), rows_x.dtype).at[position].set(rows_x)
    arrived = lax.all_to_all(outgoing, "dp", split_axis=0, concat_axis=0, tiled=True)
    preact = jnp.dot(arrived, proj_weight, preferred_element_type=jnp.float32)
    activated = jax.nn.silu(preact).astype(jnp.bfloat16)
    attended, d_acts = block_pass(activated, norm_gain, slot_user, slot_order, cotangent)
    d_acts = lax.optimization_barrier(d_acts)
    d_pre = (d_acts.astype(jnp.float32) * silu_grad(preact)).astype(jnp.bfloat16)
    d_slots = lax.dot_general(
        d_pre, proj_weight, contract_cols, preferred_element_type=jnp.float32
    ).astype(jnp.bfloat16)
    returned = lax.all_to_all(d_slots, "dp", split_axis=0, concat_axis=0, tiled=True)
    grad_tokens = returned[position]
    weight_shard = lax.psum_scatter(
        lax.dot_general(arrived, d_pre, contract_rows, preferred_element_type=jnp.float32),
        "dp",
        scatter_dimension=0,
        tiled=True,
    )
    grad_weight = lax.psum(weight_shard, "replica")
    return (attended[None], grad_tokens[None], grad_weight)


def solution(mesh):
    return jax.shard_map(
        body,
        mesh=mesh,
        in_specs=(P("replica", "dp", None), P("replica", None), P(), P(), P("replica", "dp", None)),
        out_specs=(P("replica", "dp", None), P("replica", "dp", None), P("dp", None)),
        check_vma=False,
    )
```

profile of v0, /device:TPU:2, one launch (start us, length us, event | category | flops | bytes accessed | tf_op | source)
XLA Modules:
  0.0 404.1 jit_solution(13800217942383147937)
XLA Ops:
  8.6 2.4 scatter_custom_fusion
  11.0 2.0 all_to_all.16
  13.0 18.0 %all-to-all-start = ((bf16[64,4,1024]{2,1,0:T(4,128)(2,1)}), bf16[64,4,1024]{2,1,0:T(4,128)(2,1)}, u32[]{:S(2)}, u32[]{:S(2)}) async-start(bf16[64,4,1024]{2,1,0:T(4,128)(2,1)} %all_to_all.16), calls=%async_computation | async-start | bytes 1048576 | tf_op jit(solution)/shard_map/all_to_all | solution.py:79
  33.4 15.2 %all-to-all-done = bf16[64,4,1024]{2,1,0:T(4,128)(2,1)} async-done(((bf16[64,4,1024]{2,1,0:T(4,128)(2,1)}), bf16[64,4,1024]{2,1,0:T(4,128)(2,1)}, u32[]{:S(2)}, u32[]{:S(2)}) %all-to-all-start) | async-done | bytes 524320 | tf_op jit(solution)/shard_map/all_to_all | solution.py:79
  48.6 2.0 all_to_all.18
  50.6 3.4 multiply_convert_fusion.1
  54.0 2.5 reshape.382
  56.5 2.2 fusion.27
  58.7 1.8 copy.48
  61.8 1.8 fusion.28
  63.6 2.1 copy.37
  68.6 2.4 convolution_bitcast_fusion.2
  74.4 2.3 copy.47
  76.7 5.6 %fusion.26 = f32[1024,1536]{1,0:T(8,128)} fusion(bf16[256,1024]{1,0:T(8,128)(2,1)} %all_to_all.18, f32[256,1536]{1,0:T(8,128)} %get-tuple-element.17, bf16[256,1536]{1,0:T(8,128)(2,1)} %copy.47), kind=kOutput, calls=%fused_computation.74 | convolution fusion | flops 809238528 | bytes 9175040 | tf_op jit(solution)/shard_map/dot_general | solution.py:91
  82.4 3.6 convolution_convert_fusion
  86.0 2.1 all_to_all.19
  88.1 6.0 %all-to-all-start.1 = ((bf16[64,4,1024]{2,1,0:T(4,128)(2,1)}), bf16[64,4,1024]{2,1,0:T(4,128)(2,1)}, u32[]{:S(2)}, u32[]{:S(2)}) async-start(bf16[64,4,1024]{2,1,0:T(4,128)(2,1)} %all_to_all.19), calls=%async_computation.1 | async-start | bytes 1048576 | tf_op jit(solution)/shard_map/all_to_all | solution.py:88
  94.2 2.0 copy.35
  96.2 153.9 %reduce-scatter.2.cloned.1.call-done = f32[16,1536]{1,0:T(8,128)} async-done(((f32[1024,1536]{1,0:T(8,128)}), f32[16,1536]{1,0:T(8,128)}) %reduce-scatter.2.cloned.1.call-update) | async-done | bytes 98320 | tf_op jit(solution)/shard_map/reduce_scatter | solution.py:90
  250.1 1.9 multiply_convert_fusion.2
  252.0 2.0 all_to_all.21
  254.0 2.9 gather_fusion
  256.8 138.8 %all-reduce.5.cloned.1.call-done = f32[16,1536]{1,0:T(8,128)} async-done(((f32[16,1536]{1,0:T(8,128)}), f32[16,1536]{1,0:T(8,128)}) %all-reduce.5.cloned.1.call-update) | async-done | bytes 98320 | tf_op jit(solution)/shard_map/psum | solution.py:96
  395.7 1.5 copy.58
  (56 shorter events, 11.3 us)
Async XLA Ops:
  7.2 43.4 %copy-start = (bf16[1024,1536]{1,0:T(8,128)(2,1)S(1)}, bf16[1024,1536]{1,0:T(8,128)(2,1)}, u32[]{:S(2)}) copy-start(bf16[1024,1536]{1,0:T(8,128)(2,1)} %param.7) | copy-start | bytes 9437188
  8.1 23.1 %copy-start.9 = (s32[1,8192]{1,0:T(1,128)S(1)}, s32[1,8192]{1,0:T(1,128)}, u32[]{:S(2)}) copy-start(s32[1,8192]{1,0:T(1,128)} %param.6) | copy-start | bytes 98308
  8.6 23.7 %copy-start.4 = (bf16[1,256,512]{2,1,0:T(8,128)(2,1)S(1)}, bf16[1,256,512]{2,1,0:T(8,128)(2,1)}, u32[]{:S(2)}) copy-start(bf16[1,256,512]{2,1,0:T(8,128)(2,1)} %param.9) | copy-start | bytes 786436
  13.0 35.6 %all-to-all-start = ((bf16[64,4,1024]{2,1,0:T(4,128)(2,1)}), bf16[64,4,1024]{2,1,0:T(4,128)(2,1)}, u32[]{:S(2)}, u32[]{:S(2)}) async-start(bf16[64,4,1024]{2,1,0:T(4,128)(2,1)} %all_to_all.16), calls=%async_computation | async-start | bytes 1048576 | tf_op jit(solution)/shard_map/all_to_all | solution.py:79
  31.1 219.1 %reduce-scatter.2.cloned.1.call-start = ((), (), s32[]{:S(2)}) async-start(), calls=%async_computation.3 | async-start | bytes 6389760 | tf_op jit(solution)/shard_map/reduce_scatter | solution.py:90
  60.5 1.3 copy-start.7
  61.8 1.8 copy-start.5
  61.8 3.9 copy-start.10
  65.7 2.8 copy-start.1
  65.7 2.9 copy-start.3
  68.5 2.5 copy-start.6
  68.5 2.5 copy-start.8
  71.0 1.1 copy-start.2
  88.1 164.0 %all-to-all-start.1 = ((bf16[64,4,1024]{2,1,0:T(4,128)(2,1)}), bf16[64,4,1024]{2,1,0:T(4,128)(2,1)}, u32[]{:S(2)}, u32[]{:S(2)}) async-start(bf16[64,4,1024]{2,1,0:T(4,128)(2,1)} %all_to_all.19), calls=%async_computation.1 | async-start | bytes 1048576 | tf_op jit(solution)/shard_map/all_to_all | solution.py:88
  94.1 301.6 %all-reduce.5.cloned.1.call-start = ((), (), s32[]{:S(2)}) async-start(), calls=%async_computation.4 | async-start | bytes 196608 | tf_op jit(solution)/shard_map/psum | solution.py:96
Sparse Core Ops, SparseCore 0:
  82.5 167.5 reduce-scatter.1
  252.4 143.1 all-reduce.4
where the time goes:
time: 405 us; the launch traced here: 404 us
  waiting for transfers between devices  308 us (76%)
  local copies, waits for them, and re-layouts  29.1 us (7%)
  starting transfers between devices  24.3 us (6%)
  matrix products  20.5 us (5%)
  between operations  14.3 us (4%)
  other arithmetic  7.8 us (2%)
    reduce_scatter x1, waiting for transfers between devices, body(): lax.psum_scatter(lax.dot_general(arrived, d_pre, contract_rows, preferred...  154 us
    psum x1, waiting for transfers between devices, body(): grad_weight = lax.psum(weight_shard, 'replica')  139 us
    all_to_all x1, starting transfers between devices, body(): lax.all_to_all(outgoing, 'dp', split_axis=0, concat_axis=0, tiled=True)  18 us
    all_to_all x1, waiting for transfers between devices, body(): lax.all_to_all(outgoing, 'dp', split_axis=0, concat_axis=0, tiled=True)  15.2 us
  transfers between devices with their start and end apart: 4, of which 3 were waited for; matrix products, arithmetic and copies ran while one was open for 3% of the time, Pallas kernels for 0%

commit v1 on v0

v1 whole, which is shorter than its diff:
```python
import functools

import jax
import jax.numpy as jnp
from jax import lax
from jax.experimental import pallas as pl
from jax.experimental.pallas import tpu as pltpu
from jax.sharding import PartitionSpec as P

HEADS = 4
HEAD_DIM = 128
MESH = pl.DeviceIdType.MESH
F32 = jnp.float32
BF16 = jnp.bfloat16


def dot(a, b, ca=1, cb=0):
    return lax.dot_general(a, b, (((ca,), (cb,)), ((), ())), preferred_element_type=F32)


def iota(shape, dim):
    return lax.broadcasted_iota(jnp.int32, shape, dim)


def split(x):
    high = x.astype(BF16)
    return high, (x - high.astype(F32)).astype(BF16)


def kernel(
    n, depth, users, tok, gain, w_hbm, gout_hbm, att_hbm, gtok, gw,
    w, gout, att, out1, in1, out2, in2, arrived, slots, pick, pick_t, mix, mix_t, perm,
    turned, turned_in, act, slope, dpre, dpre_in, vis, scores, gates, mixed, dmixed,
    grad, ring_out, ring_in, total, plane_out, plane_in, final,
    load_sem, a2a_send, a2a_recv, pair_send, pair_recv, ring_send, ring_recv, tail_send, tail_recv,
):
    me = lax.axis_index("dp")
    z = lax.axis_index("replica")
    rows, width = tok.shape
    qkv = w.shape[1]
    hw = gout.shape[1]
    core = lax.rem(me, 2)
    chip = me // 2
    chips = n // 2
    half = depth // 2
    partner = me + 1 - 2 * core

    barrier = pltpu.get_barrier_semaphore()

    @pl.loop(1, n)
    def _(k):
        pl.semaphore_signal(barrier, inc=1, device_id=(lax.rem(me + k, n), z), device_id_type=MESH)

    @pl.loop(1, depth)
    def _(k):
        pl.semaphore_signal(barrier, inc=1, device_id=(me, lax.rem(z + k, depth)), device_id_type=MESH)

    load_w = pltpu.make_async_copy(w_hbm, w, load_sem.at[0])
    load_g = pltpu.make_async_copy(gout_hbm, gout, load_sem.at[1])
    load_w.start()
    load_g.start()

    r0, r1 = iota((rows, rows), 0), iota((rows, rows), 1)
    diag = r0 == r1
    owner_row = (users[pl.ds(me, 1), :] >> 2).astype(F32)
    owner_col = jnp.sum(jnp.where(diag, owner_row, 0.0), axis=1, keepdims=True)
    rank = jnp.sum(jnp.where((owner_col == owner_row) & (r0 < r1), 1.0, 0.0), axis=0, keepdims=True)
    place = owner_row * 4.0 + rank
    place_col = jnp.sum(jnp.where(diag, place, 0.0), axis=1, keepdims=True)
    pick[...] = jnp.where(iota((256, rows), 0).astype(F32) == place, 1.0, 0.0).astype(BF16)
    pick_t[...] = jnp.where(iota((rows, 256), 1).astype(F32) == place_col, 1.0, 0.0).astype(BF16)
    m0, m1 = iota((256, 256), 0), iota((256, 256), 1)
    mix[...] = jnp.where(m1 == ((m0 & 63) >> 2) * 16 + (m0 >> 6) * 4 + (m0 & 3), 1.0, 0.0).astype(BF16)
    mix_t[...] = jnp.where(m0 == ((m1 & 63) >> 2) * 16 + (m1 >> 6) * 4 + (m1 & 3), 1.0, 0.0).astype(BF16)

    def unpack(blocks, flat):
        for g in range(4):
            rows_g = dot(mix[...], blocks[g * 16:(g + 1) * 16].reshape(256, 256)).astype(BF16)
            for q in range(4):
                flat[g * 64:(g + 1) * 64, q * 256:(q + 1) * 256] = rows_g[q * 64:(q + 1) * 64]

    def pack(flat, blocks):
        for g in range(4):
            rows_g = jnp.concatenate(
                [flat[g * 64:(g + 1) * 64, q * 256:(q + 1) * 256] for q in range(4)], axis=0
            )
            blocks[g * 16:(g + 1) * 16] = dot(mix_t[...], rows_g).astype(BF16).reshape(16, 16, 256)

    slots[...] = dot(pick[...], tok[...]).astype(BF16)
    pack(slots, out1)

    pl.semaphore_wait(barrier, n - 1 + depth - 1)

    def exchange(source, target, index):
        @pl.loop(1, n)
        def _(k):
            peer = lax.rem(me + k, n)
            pltpu.make_async_remote_copy(
                source.at[peer], target.at[me], a2a_send.at[index], a2a_recv.at[index],
                device_id=(peer, z), device_id_type=MESH,
            ).start()

        target[pl.ds(me, 1)] = source[pl.ds(me, 1)]

    def whole(source, target, sends, recvs, index, count):
        return pltpu.make_async_remote_copy(
            source.at[pl.ds(0, count)], target.at[pl.ds(0, count)], sends.at[index], recvs.at[index],
            device_id=(partner, z), device_id_type=MESH,
        )

    exchange(out1, in1, 0)

    everyone = users[...]
    inbound = jnp.where((everyone >> 2) == me, 1.0, 0.0).astype(BF16)
    upto = jnp.where(r0 <= r1, 1.0, 0.0).astype(BF16)
    count = dot(inbound, upto).astype(BF16)
    spread = jnp.where((iota((256, n), 0) >> 2) == iota((256, n), 1), 1.0, 0.0).astype(BF16)
    nth = ((iota((256, rows), 0) & 3) + 1).astype(F32)
    match = (dot(spread, inbound) > 0.5) & (dot(spread, count) == nth)
    named = dot(spread, (everyone + 1).astype(F32).astype(BF16))
    user_col = jnp.sum(jnp.where(match, named, 0.0), axis=1, keepdims=True) - 1.0
    user_row = jnp.sum(jnp.where(m0 == m1, user_col, 0.0), axis=0, keepdims=True)
    vis[...] = jnp.where((user_col == user_row) & (user_col >= 0.0) & (m1 <= m0), 1.0, 0.0)

    @pl.loop(0, 4)
    def _(t):
        d0 = iota((256, width), 0) + t * 256
        want = (((d0 & 31) * 2 + (d0 >> 9)) << 4) + ((d0 >> 5) & 15)
        perm[pl.ds(pl.multiple_of(t * 256, 256), 256), :] = jnp.where(
            iota((256, width), 1) == want, 1.0, 0.0
        ).astype(BF16)

    load_w.wait()
    load_g.wait()
    whole(out1, in1, a2a_send, a2a_recv, 0, n - 1).wait_recv()
    unpack(in1, arrived)

    @pl.loop(0, 3)
    def _(t):
        cols = pl.ds(pl.multiple_of(t * 512, 512), 512)
        pre = dot(arrived[...], w[:, cols])
        sig = jax.nn.sigmoid(pre)
        act[:, cols] = (pre * sig).astype(BF16)
        slope[:, cols] = sig * (1.0 + pre * (1.0 - sig))

    for t in range(4):
        turned[t // 2, (t % 2) * 256:(t % 2 + 1) * 256, :] = dot(
            perm[t * 256:(t + 1) * 256, :], arrived[...], 1, 1
        ).astype(BF16)
    swap_rows = pltpu.make_async_remote_copy(
        turned.at[1 - core], turned_in, pair_send.at[0], pair_recv.at[0],
        device_id=(partner, z), device_id_type=MESH,
    )
    swap_rows.start()

    scale = HEAD_DIM ** (-0.5)
    seen = vis[...] > 0.5
    for h in range(HEADS):
        q_cols = slice(h * HEAD_DIM, (h + 1) * HEAD_DIM)
        k_cols = slice(hw + h * HEAD_DIM, hw + (h + 1) * HEAD_DIM)
        v_cols = slice(2 * hw + h * HEAD_DIM, 2 * hw + (h + 1) * HEAD_DIM)
        score = dot(act[:, q_cols], act[:, k_cols], 1, 1) * scale
        sig = jax.nn.sigmoid(score)
        weight = jnp.where(seen, score * sig, 0.0)
        scores[h] = weight
        gates[h] = jnp.where(seen, sig * (1.0 + score * (1.0 - sig)) * scale, 0.0)
        high, low = split(weight)
        values = act[:, v_cols]
        mixed[:, q_cols] = dot(high, values) + dot(low, values)

    x = mixed[...]
    center = x - jnp.mean(x, axis=1, keepdims=True)
    scaling = lax.rsqrt(jnp.mean(center * center, axis=1, keepdims=True) + 1e-06)
    hat = center * scaling
    att[...] = (hat * gain[...]).astype(BF16)
    store_att = pltpu.make_async_copy(att, att_hbm, load_sem.at[2])
    store_att.start()
    d_hat = gout[...].astype(F32) * gain[...]
    d_center = scaling * (d_hat - hat * jnp.mean(d_hat * hat, axis=1, keepdims=True))
    dmixed[...] = d_center - jnp.mean(d_center, axis=1, keepdims=True)

    for h in range(HEADS):
        q_cols = slice(h * HEAD_DIM, (h + 1) * HEAD_DIM)
        k_cols = slice(hw + h * HEAD_DIM, hw + (h + 1) * HEAD_DIM)
        v_cols = slice(2 * hw + h * HEAD_DIM, 2 * hw + (h + 1) * HEAD_DIM)
        values = act[:, v_cols]
        m_high, m_low = split(dmixed[:, q_cols])
        d_score = (dot(m_high, values, 1, 1) + dot(m_low, values, 1, 1)) * gates[h]
        s_high, s_low = split(d_score)
        w_high, w_low = split(scores[h])
        keys, queries = act[:, k_cols], act[:, q_cols]
        parts = (
            (q_cols, dot(s_high, keys) + dot(s_low, keys)),
            (k_cols, dot(s_high, queries, 0, 0) + dot(s_low, queries, 0, 0)),
            (v_cols, dot(w_high, m_high, 0, 0) + dot(w_high, m_low, 0, 0) + dot(w_low, m_high, 0, 0)),
        )
        for cols, value in parts:
            dpre[:, cols] = (value.astype(BF16).astype(F32) * slope[:, cols]).astype(BF16)

    swap_dpre = pltpu.make_async_remote_copy(
        dpre, dpre_in, pair_send.at[1], pair_recv.at[1], device_id=(partner, z), device_id_type=MESH
    )
    swap_dpre.start()

    for t in range(4):
        slots[:, t * 256:(t + 1) * 256] = dot(dpre[...], w[t * 256:(t + 1) * 256, :], 1, 1).astype(BF16)
    pack(slots, out2)
    exchange(out2, in2, 1)

    swap_rows.wait()
    swap_dpre.wait()
    column_halves = 2
    wide = qkv // column_halves

    @pl.loop(0, depth // 4)
    def _(b):
        band = pl.ds(pl.multiple_of(b * 4 * chips, 4 * chips), 4 * chips)
        own = turned[pl.ds(core, 1), band, :].reshape(4 * chips, 256)
        other = turned_in[band, :]
        for c in range(column_halves):
            cols = slice(c * wide, (c + 1) * wide)
            block = dot(own, dpre[:, cols]) + dot(other, dpre_in[:, cols])
            grad[pl.ds(b * 4, 4), c] = block.reshape(4, chips, wide)

    def piece(ref, lead, p):
        return ref.at[(*lead, p // 2, pl.ds((p % 2) * 16, 16))]

    def hop(direction, s, p, has_in):
        chunk = lax.rem(z + half - s, depth) if direction == 0 else lax.rem(z + half + s, depth)
        to = lax.rem(z + 1, depth) if direction == 0 else lax.rem(z + depth - 1, depth)
        value = piece(grad, (chunk,), p)[...]
        if has_in:
            arrive(direction, s - 1, p)
            value = value + piece(ring_in, (direction, s - 1), p)[...].astype(F32)
        piece(ring_out, (direction, s), p)[...] = value.astype(BF16)
        pltpu.make_async_remote_copy(
            piece(ring_out, (direction, s), p), piece(ring_in, (direction, s), p),
            ring_send.at[direction, s, p], ring_recv.at[direction, s, p],
            device_id=(me, to), device_id_type=MESH,
        ).start()

    def arrive(direction, s, p):
        pltpu.make_async_remote_copy(
            piece(ring_out, (direction, s), p), piece(ring_in, (direction, s), p),
            ring_send.at[direction, s, p], ring_recv.at[direction, s, p],
            device_id=(me, z), device_id_type=MESH,
        ).wait_recv()

    def sent(direction, s, p):
        pltpu.make_async_remote_copy(
            piece(ring_out, (direction, s), p), piece(ring_in, (direction, s), p),
            ring_send.at[direction, s, p], ring_recv.at[direction, s, p],
            device_id=(me, z), device_id_type=MESH,
        ).wait_send()

    first = ((0, 1), (2, 3))
    for i in range(2):
        for direction in range(2):
            hop(direction, 0, first[direction][i], False)
    for direction in range(2):
        for p in first[1 - direction]:
            hop(direction, 1, p, False)
    for i in range(2):
        for direction in range(2):
            hop(direction, 1, first[direction][i], True)

    @pl.loop(2, half)
    def _(s):
        for p in range(4):
            for direction in range(2):
                hop(direction, s, p, True)

    for p in range(4):
        value = piece(grad, (z,), p)[...]
        for direction in range(2):
            arrive(direction, half - 1, p)
            value = value + piece(ring_in, (direction, half - 1), p)[...].astype(F32)
        total[(p % 2) * 16:(p % 2 + 1) * 16, (p // 2) * wide:(p // 2 + 1) * wide] = value

    for i in range(chips):
        plane_out[i] = total[i:i + 1, :]

    @pl.loop(1, chips)
    def _(k):
        to = lax.rem(chip + k, chips)
        pltpu.make_async_remote_copy(
            plane_out.at[to], plane_in.at[chip], tail_send.at[0], tail_recv.at[0],
            device_id=(to * 2 + core, z), device_id_type=MESH,
        ).start()

    plane_in[pl.ds(chip, 1)] = plane_out[pl.ds(chip, 1)]

    whole(out2, in2, a2a_send, a2a_recv, 1, n - 1).wait_recv()
    unpack(in2, arrived)
    gtok[...] = dot(pick_t[...], arrived[...]).astype(BF16)

    whole(plane_out, plane_in, tail_send, tail_recv, 0, chips - 1).wait_recv()
    row = plane_in[0]
    for i in range(1, chips):
        row = row + plane_in[i]
    final[pl.ds(z, 1)] = row.reshape(1, 1, qkv)

    @pl.loop(1, depth)
    def _(k):
        pltpu.make_async_remote_copy(
            final.at[z], final.at[z], tail_send.at[1], tail_recv.at[1],
            device_id=(me, lax.rem(z + k, depth)), device_id_type=MESH,
        ).start()

    whole(out1, in1, a2a_send, a2a_recv, 0, n - 1).wait_send()
    whole(out2, in2, a2a_send, a2a_recv, 1, n - 1).wait_send()
    whole(plane_out, plane_in, tail_send, tail_recv, 0, chips - 1).wait_send()
    for direction in range(2):
        for p in first[direction]:
            sent(direction, 0, p)

    @pl.loop(1, half)
    def _(s):
        for direction in range(2):
            for p in range(4):
                sent(direction, s, p)

    store_att.wait()
    whole(final, final, tail_send, tail_recv, 1, depth - 1).wait()
    for i in range(depth):
        gw[i:i + 1, :] = final[i]


def body(tokens, user_of_row, proj_weight, norm_gain, grad_out):
    n = lax.axis_size("dp")
    depth = lax.axis_size("replica")
    rows, width = tokens.shape[1:]
    qkv = proj_weight.shape[1]
    slots, hw = grad_out.shape[1:]
    chips, half = n // 2, depth // 2
    vmem = pl.BlockSpec(memory_space=pltpu.VMEM)
    anywhere = pl.BlockSpec(memory_space=pl.ANY)
    blocks = pltpu.VMEM((n, 16, 256), BF16)
    ring = pltpu.VMEM((2, half, 2, chips, qkv // 2), BF16)
    dma = pltpu.SemaphoreType.DMA
    attended, grad_tokens, grad_weight = pl.pallas_call(
        functools.partial(kernel, n, depth),
        out_shape=(
            jax.ShapeDtypeStruct((slots, hw), BF16),
            jax.ShapeDtypeStruct((rows, width), BF16),
            jax.ShapeDtypeStruct((width // n, qkv), F32),
        ),
        in_specs=[vmem, vmem, vmem, anywhere, anywhere],
        out_specs=(anywhere, vmem, vmem),
        scratch_shapes=[
            pltpu.VMEM((width, qkv), BF16),
            pltpu.VMEM((slots, hw), BF16),
            pltpu.VMEM((slots, hw), BF16),
            blocks, blocks, blocks, blocks,
            pltpu.VMEM((slots, width), BF16),
            pltpu.VMEM((slots, width), BF16),
            pltpu.VMEM((slots, rows), BF16),
            pltpu.VMEM((rows, slots), BF16),
            pltpu.VMEM((256, 256), BF16),
            pltpu.VMEM((256, 256), BF16),
            pltpu.VMEM((width, width), BF16),
            pltpu.VMEM((2, width // 2, slots), BF16),
            pltpu.VMEM((width // 2, slots), BF16),
            pltpu.VMEM((slots, qkv), BF16),
            pltpu.VMEM((slots, qkv), F32),
            pltpu.VMEM((slots, qkv), BF16),
            pltpu.VMEM((slots, qkv), BF16),
            pltpu.VMEM((slots, slots), F32),
            pltpu.VMEM((HEADS, slots, slots), F32),
            pltpu.VMEM((HEADS, slots, slots), F32),
            pltpu.VMEM((slots, hw), F32),
            pltpu.VMEM((slots, hw), F32),
            pltpu.VMEM((depth, 2, chips, qkv // 2), F32),
            ring, ring,
            pltpu.VMEM((chips, qkv), F32),
            pltpu.VMEM((chips, 1, qkv), F32),
            pltpu.VMEM((chips, 1, qkv), F32),
            pltpu.VMEM((depth, 1, qkv), F32),
            dma((3,)), dma((2,)), dma((2,)), dma((2,)), dma((2,)),
            dma((2, half, 4)), dma((2, half, 4)), dma((2,)), dma((2,)),
        ],
        compiler_params=pltpu.CompilerParams(
            collective_id=0, has_side_effects=True, vmem_limit_bytes=60 * 1024 * 1024
        ),
    )(
        user_of_row.reshape(n, rows),
        tokens[0],
        norm_gain.reshape(1, hw),
        proj_weight,
        grad_out[0],
    )
    return (attended[None], grad_tokens[None], grad_weight)


def solution(mesh):
    return jax.shard_map(
        body,
        mesh=mesh,
        in_specs=(P("replica", "dp", None), P("replica", None), P(), P(), P("replica", "dp", None)),
        out_specs=(P("replica", "dp", None), P("replica", "dp", None), P("dp", None)),
        check_vma=False,
    )
```

time: 405 us -> 98.7 us (0.24)
  waiting for transfers between devices: 308 us -> 0 us
  Pallas kernels: 0 us -> 92.9 us
  starting transfers between devices: 24.3 us -> 0 us
  local copies, waits for them, and re-layouts: 29.1 us -> 4.88 us
  matrix products: 20.5 us -> 0 us
  between operations: 14.3 us -> 0.64 us
  other arithmetic: 7.8 us -> 0 us
    reduce_scatter x1 -> x0, waiting for transfers between devices: 154 us -> none  [body(): lax.psum_scatter(lax.dot_general(arrived, d_pre, contract_rows, preferred...]
    psum x1 -> x0, waiting for transfers between devices: 139 us -> none  [body(): grad_weight = lax.psum(weight_shard, 'replica')]
    pallas_call x0 -> x1, Pallas kernels: none -> 92.9 us  [body(): pl.pallas_call(functools.partial(kernel, n, depth), out_shape=(jax.ShapeD...]
    all_to_all x2 -> x0, starting transfers between devices: 24 us -> none  [the longest x1 18 us: body(): lax.all_to_all(outgoing, 'dp', split_axis=0, concat_axis=0, tiled=True)]
    dot_general x9 -> x0, matrix products: 20.5 us -> none  [the longest x1 5.6 us: body(): lax.dot_general(arrived, d_pre, contract_rows, preferred_element_type=jnp...]
    all_to_all x2 -> x0, waiting for transfers between devices: 15.2 us -> none  [the longest x1 15.2 us: body(): lax.all_to_all(outgoing, 'dp', split_axis=0, concat_axis=0, tiled=True)]
    all_to_all x4 -> x0, local copies, waits for them, and re-layouts: 8.05 us -> none  [the longest x2 4.04 us: body(): lax.all_to_all(outgoing, 'dp', split_axis=0, concat_axis=0, tiled=True)]
    reshape x3 -> x0, local copies, waits for them, and re-layouts: 6.54 us -> none  [the longest x2 4.09 us: attend(): jnp.einsum('hqk,khd->qhd', weights, values, precision=lax.Precision.HIGHEST)]
  transfers between devices with their start and end apart: 4 -> 0, of which waited for: 3 -> 0; matrix products, arithmetic and copies ran while one was open for 3% -> 0% of each run, Pallas kernels for 0% -> 0%
where the time goes in v1:
time: 98.7 us; the launch traced here: 98.5 us
  Pallas kernels  92.9 us (94%)
  local copies, waits for them, and re-layouts  4.88 us (5%)
    pallas_call x1, Pallas kernels, body(): pl.pallas_call(functools.partial(kernel, n, depth), out_shape=(jax.ShapeD...  92.9 us
    unnamed x3, local copies, waits for them, and re-layouts  4.88 us

profile of v1, /device:TPU:2, one launch (start us, length us, event | category | flops | bytes accessed | tf_op | source)
XLA Modules:
  0.0 98.5 jit_solution(5751911034166573121)
XLA Ops:
  0.6 92.9 %shard_map.76 = (bf16[256,512]{1,0:T(8,128)(2,1)}, bf16[128,1024]{1,0:T(8,128)(2,1)}, f32[16,1536]{1,0:T(8,128)}) custom-call(s32[64,128]{1,0:T(8,128)} %bitcast.10, bf16[128,1024]{1,0:T(8,128)(2,1)} %bitcast.6, f32[1,512]{1,0:T(1,128)} %bitcast.11, bf16[1024,1536]{1,0:T(8,128)(2,1)} %w_hbm.1, bf16[256,512]{1,0:T(8,128)(2,1)} %bitcast.7), custom_call_target="tpu_custom_call" | custom-call | tf_op jit(solution)/shard_map/pallas_call | solution.py:341
  93.6 1.7 %copy.11 = bf16[1,256,512]{2,1,0:T(8,128)(2,1)} copy(bf16[1,256,512]{2,1,0:T(8,128)(2,1)} %bitcast.9) | data formatting | bytes 524288
  95.2 1.7 %copy.12 = bf16[1,128,1024]{2,1,0:T(8,128)(2,1)} copy(bf16[1,128,1024]{2,1,0:T(8,128)(2,1)} %bitcast.8) | data formatting | bytes 524288
  96.9 1.5 %copy.13 = f32[16,1536]{1,0:T(8,128)} copy(f32[16,1536]{1,0:T(8,128)} %get-tuple-element.14) | data formatting | bytes 196608

commit v2 on v1

--- a/solution.py
+++ b/solution.py
@@ -28,8 +28,8 @@
 
 
 def kernel(
-    n, depth, users, tok, gain, w_hbm, gout_hbm, att_hbm, gtok, gw,
-    w, gout, att, out1, in1, out2, in2, arrived, slots, pick, pick_t, mix, mix_t, perm,
+    n, depth, users_hbm, tok_hbm, gain_hbm, w_hbm, gout_hbm, att, gtok, gw,
+    users, tok, gain, w, gout, out1, in1, out2, in2, arrived, slots, pick, pick_t, mix, mix_t, perm,
     turned, turned_in, act, slope, dpre, dpre_in, vis, scores, gates, mixed, dmixed,
     grad, ring_out, ring_in, total, plane_out, plane_in, final,
     load_sem, a2a_send, a2a_recv, pair_send, pair_recv, ring_send, ring_recv, tail_send, tail_recv,
@@ -55,11 +55,12 @@
     def _(k):
         pl.semaphore_signal(barrier, inc=1, device_id=(me, lax.rem(z + k, depth)), device_id_type=MESH)
 
-    load_w = pltpu.make_async_copy(w_hbm, w, load_sem.at[0])
-    load_g = pltpu.make_async_copy(gout_hbm, gout, load_sem.at[1])
-    load_w.start()
-    load_g.start()
-
+    pairs = ((users_hbm, users), (tok_hbm, tok), (gain_hbm, gain), (w_hbm, w), (gout_hbm, gout))
+    loads = [pltpu.make_async_copy(a, b, load_sem.at[i]) for i, (a, b) in enumerate(pairs)]
+    for load in loads:
+        load.start()
+
+    loads[0].wait()
     r0, r1 = iota((rows, rows), 0), iota((rows, rows), 1)
     diag = r0 == r1
     owner_row = (users[pl.ds(me, 1), :] >> 2).astype(F32)
@@ -86,17 +87,18 @@
             )
             blocks[g * 16:(g + 1) * 16] = dot(mix_t[...], rows_g).astype(BF16).reshape(16, 16, 256)
 
+    loads[1].wait()
     slots[...] = dot(pick[...], tok[...]).astype(BF16)
     pack(slots, out1)
 
     pl.semaphore_wait(barrier, n - 1 + depth - 1)
 
-    def exchange(source, target, index):
+    def exchange(source, target, index, recv):
         @pl.loop(1, n)
         def _(k):
-            peer = lax.rem(me + k, n)
+            peer = me ^ (n - k)
             pltpu.make_async_remote_copy(
-                source.at[peer], target.at[me], a2a_send.at[index], a2a_recv.at[index],
+                source.at[peer], target.at[me], a2a_send.at[index], a2a_recv.at[recv],
                 device_id=(peer, z), device_id_type=MESH,
             ).start()
 
@@ -108,7 +110,8 @@
             device_id=(partner, z), device_id_type=MESH,
         )
 
-    exchange(out1, in1, 0)
+    near = me // (n // 2)
+    exchange(out1, in1, 0, near)
 
     everyone = users[...]
     inbound = jnp.where((everyone >> 2) == me, 1.0, 0.0).astype(BF16)
@@ -130,23 +133,41 @@
             iota((256, width), 1) == want, 1.0, 0.0
         ).astype(BF16)
 
-    load_w.wait()
-    load_g.wait()
-    whole(out1, in1, a2a_send, a2a_recv, 0, n - 1).wait_recv()
-    unpack(in1, arrived)
-
-    @pl.loop(0, 3)
-    def _(t):
-        cols = pl.ds(pl.multiple_of(t * 512, 512), 512)
-        pre = dot(arrived[...], w[:, cols])
-        sig = jax.nn.sigmoid(pre)
-        act[:, cols] = (pre * sig).astype(BF16)
-        slope[:, cols] = sig * (1.0 + pre * (1.0 - sig))
-
-    for t in range(4):
-        turned[t // 2, (t % 2) * 256:(t % 2 + 1) * 256, :] = dot(
-            perm[t * 256:(t + 1) * 256, :], arrived[...], 1, 1
-        ).astype(BF16)
+    loads[3].wait()
+
+    def project(half_of_plane):
+        band = pl.ds(pl.multiple_of(half_of_plane * 128, 128), 128)
+        for g in range(2):
+            blocks_g = in1[pl.ds(half_of_plane * 32 + g * 16, 16)].reshape(256, 256)
+            rows_g = dot(mix[...], blocks_g).astype(BF16)
+            to = pl.ds(pl.multiple_of(half_of_plane * 128 + g * 64, 64), 64)
+            for q in range(4):
+                arrived[to, q * 256:(q + 1) * 256] = rows_g[q * 64:(q + 1) * 64]
+
+        @pl.loop(0, 3)
+        def _(t):
+            cols = pl.ds(pl.multiple_of(t * 512, 512), 512)
+            pre = dot(arrived[band, :], w[:, cols])
+            sig = jax.nn.sigmoid(pre)
+            act[band, cols] = (pre * sig).astype(BF16)
+            slope[band, cols] = sig * (1.0 + pre * (1.0 - sig))
+
+        for t in range(4):
+            turned[t // 2, (t % 2) * 256:(t % 2 + 1) * 256, band] = dot(
+                perm[t * 256:(t + 1) * 256, :], arrived[band, :], 1, 1
+            ).astype(BF16)
+
+    def landed(recv, count):
+        pltpu.make_async_remote_copy(
+            out1.at[pl.ds(0, count)], in1.at[pl.ds(0, count)], a2a_send.at[0], a2a_recv.at[recv],
+            device_id=(partner, z), device_id_type=MESH,
+        ).wait_recv()
+
+    landed(1 - near, n // 2)
+    project(1 - near)
+    landed(near, n // 2 - 1)
+    project(near)
+
     swap_rows = pltpu.make_async_remote_copy(
         turned.at[1 - core], turned_in, pair_send.at[0], pair_recv.at[0],
         device_id=(partner, z), device_id_type=MESH,
@@ -172,13 +193,14 @@
     center = x - jnp.mean(x, axis=1, keepdims=True)
     scaling = lax.rsqrt(jnp.mean(center * center, axis=1, keepdims=True) + 1e-06)
     hat = center * scaling
+    loads[2].wait()
+    loads[4].wait()
     att[...] = (hat * gain[...]).astype(BF16)
-    store_att = pltpu.make_async_copy(att, att_hbm, load_sem.at[2])
-    store_att.start()
     d_hat = gout[...].astype(F32) * gain[...]
     d_center = scaling * (d_hat - hat * jnp.mean(d_hat * hat, axis=1, keepdims=True))
     dmixed[...] = d_center - jnp.mean(d_center, axis=1, keepdims=True)
 
+    swaps = [swap_rows]
     for h in range(HEADS):
         q_cols = slice(h * HEAD_DIM, (h + 1) * HEAD_DIM)
         k_cols = slice(hw + h * HEAD_DIM, hw + (h + 1) * HEAD_DIM)
@@ -196,31 +218,33 @@
         )
         for cols, value in parts:
             dpre[:, cols] = (value.astype(BF16).astype(F32) * slope[:, cols]).astype(BF16)
-
-    swap_dpre = pltpu.make_async_remote_copy(
-        dpre, dpre_in, pair_send.at[1], pair_recv.at[1], device_id=(partner, z), device_id_type=MESH
-    )
-    swap_dpre.start()
-
-    for t in range(4):
+            swap = pltpu.make_async_remote_copy(
+                dpre.at[:, cols], dpre_in.at[:, cols],
+                pair_send.at[len(swaps)], pair_recv.at[len(swaps)],
+                device_id=(partner, z), device_id_type=MESH,
+            )
+            swap.start()
+            swaps.append(swap)
+
+    def back(t):
         slots[:, t * 256:(t + 1) * 256] = dot(dpre[...], w[t * 256:(t + 1) * 256, :], 1, 1).astype(BF16)
-    pack(slots, out2)
-    exchange(out2, in2, 1)
-
-    swap_rows.wait()
-    swap_dpre.wait()
-    column_halves = 2
-    wide = qkv // column_halves
-
-    @pl.loop(0, depth // 4)
-    def _(b):
+
+    back(0)
+    for swap in swaps:
+        swap.wait()
+    wide = qkv // 2
+    quarter = qkv // 4
+
+    def product(b):
         band = pl.ds(pl.multiple_of(b * 4 * chips, 4 * chips), 4 * chips)
         own = turned[pl.ds(core, 1), band, :].reshape(4 * chips, 256)
         other = turned_in[band, :]
-        for c in range(column_halves):
+        for c in range(2):
             cols = slice(c * wide, (c + 1) * wide)
             block = dot(own, dpre[:, cols]) + dot(other, dpre_in[:, cols])
-            grad[pl.ds(b * 4, 4), c] = block.reshape(4, chips, wide)
+            for i in range(2):
+                part = block[:, i * quarter:(i + 1) * quarter]
+                grad[pl.ds(b * 4, 4), 2 * c + i] = part.reshape(4, chips, quarter)
 
     def piece(ref, lead, p):
         return ref.at[(*lead, p // 2, pl.ds((p % 2) * 16, 16))]
@@ -253,29 +277,40 @@
             device_id=(me, z), device_id_type=MESH,
         ).wait_send()
 
-    first = ((0, 1), (2, 3))
-    for i in range(2):
+    first = ((0, 1, 2, 3), (4, 5, 6, 7))
+    head = lax.rem(z + half, depth) // 4
+    product(head)
+    for i in range(4):
         for direction in range(2):
             hop(direction, 0, first[direction][i], False)
-    for direction in range(2):
-        for p in first[1 - direction]:
-            hop(direction, 1, p, False)
-    for i in range(2):
+
+    @pl.loop(1, depth // 4)
+    def _(i):
+        product(lax.rem(head + i, depth // 4))
+
+    for i in range(4):
+        for direction in range(2):
+            hop(direction, 1, first[1 - direction][i], False)
+    for t in range(1, 4):
+        back(t)
+    pack(slots, out2)
+    exchange(out2, in2, 1, 2)
+    for i in range(4):
         for direction in range(2):
             hop(direction, 1, first[direction][i], True)
 
     @pl.loop(2, half)
     def _(s):
-        for p in range(4):
+        for p in range(8):
             for direction in range(2):
                 hop(direction, s, p, True)
 
-    for p in range(4):
+    for p in range(8):
         value = piece(grad, (z,), p)[...]
         for direction in range(2):
             arrive(direction, half - 1, p)
             value = value + piece(ring_in, (direction, half - 1), p)[...].astype(F32)
-        total[(p % 2) * 16:(p % 2 + 1) * 16, (p // 2) * wide:(p // 2 + 1) * wide] = value
+        total[(p % 2) * 16:(p % 2 + 1) * 16, (p // 2) * quarter:(p // 2 + 1) * quarter] = value
 
     for i in range(chips):
         plane_out[i] = total[i:i + 1, :]
@@ -290,7 +325,10 @@
 
     plane_in[pl.ds(chip, 1)] = plane_out[pl.ds(chip, 1)]
 
-    whole(out2, in2, a2a_send, a2a_recv, 1, n - 1).wait_recv()
+    pltpu.make_async_remote_copy(
+        out2.at[pl.ds(0, n - 1)], in2.at[pl.ds(0, n - 1)], a2a_send.at[1], a2a_recv.at[2],
+        device_id=(partner, z), device_id_type=MESH,
+    ).wait_recv()
     unpack(in2, arrived)
     gtok[...] = dot(pick_t[...], arrived[...]).astype(BF16)
 
@@ -317,13 +355,25 @@
     @pl.loop(1, half)
     def _(s):
         for direction in range(2):
-            for p in range(4):
+            for p in range(8):
                 sent(direction, s, p)
 
-    store_att.wait()
     whole(final, final, tail_send, tail_recv, 1, depth - 1).wait()
     for i in range(depth):
         gw[i:i + 1, :] = final[i]
+
+
+def write(a, b, c, a_out, b_out, c_out, a_held, b_held, c_held, sem):
+    moves = ((a, a_held, a_out), (b, b_held, b_out), (c, c_held, c_out))
+    loads = [pltpu.make_async_copy(x, y, sem.at[0, i]) for i, (x, y, _) in enumerate(moves)]
+    stores = [pltpu.make_async_copy(y, x, sem.at[1, i]) for i, (_, y, x) in enumerate(moves)]
+    for load in loads:
+        load.start()
+    for load, store in zip(loads, stores):
+        load.wait()
+        store.start()
+    for store in stores:
+        store.wait()
 
 
 def body(tokens, user_of_row, proj_weight, norm_gain, grad_out):
@@ -334,22 +384,25 @@
     slots, hw = grad_out.shape[1:]
     chips, half = n // 2, depth // 2
     vmem = pl.BlockSpec(memory_space=pltpu.VMEM)
-    anywhere = pl.BlockSpec(memory_space=pl.ANY)
+    hbm = pl.BlockSpec(memory_space=pltpu.HBM)
     blocks = pltpu.VMEM((n, 16, 256), BF16)
-    ring = pltpu.VMEM((2, half, 2, chips, qkv // 2), BF16)
+    ring = pltpu.VMEM((2, half, 4, chips, qkv // 4), BF16)
     dma = pltpu.SemaphoreType.DMA
-    attended, grad_tokens, grad_weight = pl.pallas_call(
+    results = (
+        jax.ShapeDtypeStruct((slots, hw), BF16),
+        jax.ShapeDtypeStruct((rows, width), BF16),
+        jax.ShapeDtypeStruct((width // n, qkv), F32),
+    )
+    made = pl.pallas_call(
         functools.partial(kernel, n, depth),
-        out_shape=(
-            jax.ShapeDtypeStruct((slots, hw), BF16),
-            jax.ShapeDtypeStruct((rows, width), BF16),
-            jax.ShapeDtypeStruct((width // n, qkv), F32),
-        ),
-        in_specs=[vmem, vmem, vmem, anywhere, anywhere],
-        out_specs=(anywhere, vmem, vmem),
+        out_shape=results,
+        in_specs=[hbm] * 5,
+        out_specs=(vmem,) * 3,
         scratch_shapes=[
+            pltpu.VMEM((n, rows), jnp.int32),
+            pltpu.VMEM((rows, width), BF16),
+            pltpu.VMEM((1, hw), F32),
             pltpu.VMEM((width, qkv), BF16),
-            pltpu.VMEM((slots, hw), BF16),
             pltpu.VMEM((slots, hw), BF16),
             blocks, blocks, blocks, blocks,
             pltpu.VMEM((slots, width), BF16),
@@ -370,17 +423,17 @@
             pltpu.VMEM((HEADS, slots, slots), F32),
             pltpu.VMEM((slots, hw), F32),
             pltpu.VMEM((slots, hw), F32),
-            pltpu.VMEM((depth, 2, chips, qkv // 2), F32),
+            pltpu.VMEM((depth, 4, chips, qkv // 4), F32),
             ring, ring,
             pltpu.VMEM((chips, qkv), F32),
             pltpu.VMEM((chips, 1, qkv), F32),
             pltpu.VMEM((chips, 1, qkv), F32),
             pltpu.VMEM((depth, 1, qkv), F32),
-            dma((3,)), dma((2,)), dma((2,)), dma((2,)), dma((2,)),
-            dma((2, half, 4)), dma((2, half, 4)), dma((2,)), dma((2,)),
+            dma((5,)), dma((2,)), dma((3,)), dma((1 + 3 * HEADS,)), dma((1 + 3 * HEADS,)),
+            dma((2, half, 8)), dma((2, half, 8)), dma((2,)), dma((2,)),
         ],
         compiler_params=pltpu.CompilerParams(
-            collective_id=0, has_side_effects=True, vmem_limit_bytes=60 * 1024 * 1024
+            collective_id=0, has_side_effects=True, vmem_limit_bytes=66300000
         ),
     )(
         user_of_row.reshape(n, rows),
@@ -389,6 +442,14 @@
         proj_weight,
         grad_out[0],
     )
+    attended, grad_tokens, grad_weight = pl.pallas_call(
+        write,
+        out_shape=results,
+        in_specs=[hbm] * 3,
+        out_specs=(hbm,) * 3,
+        scratch_shapes=[pltpu.VMEM(r.shape, r.dtype) for r in results] + [dma((2, 3))],
+        compiler_params=pltpu.CompilerParams(vmem_limit_bytes=66300000),
+    )(*made)
     return (attended[None], grad_tokens[None], grad_weight)
 
 

time: 98.7 us -> 97.7 us (0.990)
  the two profiles are of different devices: /device:TPU:2 before, /device:TPU:16 now
where the time goes in v2:
time: 97.7 us; the launch traced here: 97.5 us
  Pallas kernels  96.8 us (99%)
    pallas_call x1, Pallas kernels, body(): pl.pallas_call(functools.partial(kernel, n, depth), out_shape=results, in...  95 us

profile of v2, /device:TPU:16, one launch (start us, length us, event | category | flops | bytes accessed | tf_op | source)
XLA Modules:
  0.0 97.5 jit_solution(11325200241334728641)
XLA Ops:
  0.6 95.0 %shard_map.76 = (bf16[256,512]{1,0:T(8,128)(2,1)}, bf16[128,1024]{1,0:T(8,128)(2,1)}, f32[16,1536]{1,0:T(8,128)}) custom-call(s32[64,128]{1,0:T(8,128)} %bitcast.8, bf16[128,1024]{1,0:T(8,128)(2,1)} %bitcast.6, f32[1,512]{1,0:T(1,128)} %bitcast.9, bf16[1024,1536]{1,0:T(8,128)(2,1)} %w_hbm.1, bf16[256,512]{1,0:T(8,128)(2,1)} %bitcast.7), custom_call_target="tpu_custom_call" | custom-call | tf_op jit(solution)/shard_map/pallas_call | solution.py:396
  95.7 1.8 %shard_map.77 = (bf16[256,512]{1,0:T(8,128)(2,1)}, bf16[128,1024]{1,0:T(8,128)(2,1)}, f32[16,1536]{1,0:T(8,128)}) custom-call(bf16[256,512]{1,0:T(8,128)(2,1)} %get-tuple-element.9.a, bf16[128,1024]{1,0:T(8,128)(2,1)} %get-tuple-element.10.b, f32[16,1536]{1,0:T(8,128)} %get-tuple-element.11.c), custom_call_target="tpu_custom_call" | custom-call | tf_op jit(solution)/shard_map/pallas_call | solution.py:445
